TPU v7x, 128 devices: a whole 4x4x4 slice. The times are simulated.
128 devices in a mesh: section: 32 (over y, x, z_lo), tensor: 4 (over z_hi, core).
Axes of the slice: x: 4, y: 4, z: 4 (z_hi: 2, z_lo: 2; z = z_hi * 2 + z_lo), core: 2. Of those that a mesh axis runs over, the one named last changes fastest.
Arguments:
- weights: bfloat16 [32, 4096, 4096], P('section', 'tensor'), may hold values from -0.09375 to 0.09375
- filters: float32 [32, 32, 128], P('section'), may hold values from -0.5 to 0.5
- down_input: bfloat16 [32, 512, 4096], P('section', 'tensor'), may hold values from -6 to 6
- down_cot: bfloat16 [32, 512, 4096], P('section', 'tensor'), may hold values from -6 to 6
- up_input: bfloat16 [32, 512, 4096], P('section', 'tensor'), may hold values from -6 to 6
- up_cot: bfloat16 [32, 512, 4096], P('section', 'tensor'), may hold values from -6 to 6
Outputs:
- weight_grad: bfloat16 [32, 4096, 4096], P('section', 'tensor')
- filter_grad: float32 [32, 32, 128], P('section')
- down_passed: bfloat16 [32, 512, 4096], P('section', 'tensor')
- up_passed: bfloat16 [32, 512, 4096], P('section', 'tensor')
All inputs are finite; a program needn't handle non-finite values.
Results may differ from a plain program's by a relative error of at most 0.014.
Values may be sent and summed in bfloat16 or wider, within the bound.
A program may use at most 192 MiB of HBM per device.

v0:
```python
import jax
import jax.numpy as jnp
from jax import lax
from jax.sharding import PartitionSpec as P

epsilon = 1e-06


def shifted(x, axis, by):
    devices = lax.axis_size(axis)
    pairs = [(i, i + by) for i in range(devices) if 0 <= i + by < devices]
    return lax.ppermute(x, axis, pairs)


def tap_tables(row_count, taps_total):
    target = jnp.arange(row_count, dtype=jnp.int32)[:, None, None]
    source = jnp.arange(row_count + taps_total - 1, dtype=jnp.int32)[None, :, None]
    lag_index = jnp.arange(taps_total, dtype=jnp.int32)[None, None, :]
    causal_table = (target + taps_total - 1 - source == lag_index).astype(jnp.float32)
    ahead_table = (source - target == lag_index).astype(jnp.float32)
    return (causal_table, ahead_table)


def banded(table, filter_taps, extended, row_count):
    group_count = filter_taps.shape[0]
    band = jnp.einsum("tuk,gk->gtu", table, filter_taps, precision=lax.Precision.HIGHEST)
    grouped = extended.reshape(extended.shape[0], extended.shape[1], group_count, -1)
    mixed_out = jnp.einsum("gtu,umgc->tmgc", band, grouped, precision=lax.Precision.HIGHEST)
    return mixed_out.reshape(row_count, extended.shape[1], extended.shape[2])


def layer_grads(inputs, cotangent, weight_rows, filter_taps, tables):
    causal_table, ahead_table = tables
    row_count = inputs.shape[0]
    group_count = filter_taps.shape[0]
    taps_total = filter_taps.shape[1]
    input_wide = inputs.astype(jnp.float32)
    inverse_rms = lax.rsqrt(jnp.mean(input_wide * input_wide, axis=2, keepdims=True) + epsilon)
    normed = input_wide * inverse_rms
    normed_b = normed.astype(jnp.bfloat16)
    feature_rows = lax.all_to_all(normed_b, "tensor", split_axis=2, concat_axis=0, tiled=True)
    selected = feature_rows
    values = lax.psum_scatter(
        jnp.einsum("tmd,de->tme", selected, weight_rows, preferred_element_type=jnp.float32).astype(
            jnp.bfloat16
        ),
        "tensor",
        scatter_dimension=0,
        tiled=True,
    ).astype(jnp.float32)
    before = shifted(
        values[row_count - (taps_total - 1) :].astype(jnp.bfloat16), "tensor", 1
    ).astype(jnp.float32)
    extended = jnp.concatenate([before, values], axis=0)
    convolved = banded(causal_table, filter_taps, extended, row_count)
    cot_wide = cotangent.astype(jnp.float32)
    grad_mix = cot_wide * normed
    following = shifted(grad_mix[: taps_total - 1], "tensor", -1)
    grad_ext = jnp.concatenate([grad_mix, following], axis=0)
    grad_values = banded(ahead_table, filter_taps, grad_ext, row_count)
    grad_grouped = grad_mix.reshape(row_count, grad_mix.shape[1], group_count, -1)
    ext_grouped = extended.reshape(extended.shape[0], extended.shape[1], group_count, -1)
    pairs = jnp.einsum("tmgc,umgc->gtu", grad_grouped, ext_grouped, precision=lax.Precision.HIGHEST)
    tap_part = jnp.einsum("gtu,tuk->gk", pairs, causal_table, precision=lax.Precision.HIGHEST)
    grad_values_b = grad_values.astype(jnp.bfloat16)
    shard_rows = lax.all_gather(grad_values_b, "tensor", axis=0, tiled=True)
    selected = feature_rows
    weight_sum = jnp.einsum("tmd,tme->de", selected, shard_rows, preferred_element_type=jnp.float32)
    returned_rows = jnp.einsum(
        "tme,de->tmd", shard_rows, weight_rows, preferred_element_type=jnp.float32
    )
    back_tokens = lax.all_to_all(
        returned_rows.astype(jnp.bfloat16), "tensor", split_axis=0, concat_axis=2, tiled=True
    ).astype(returned_rows.dtype)
    grad_total = cot_wide * convolved + back_tokens
    projection_mean = jnp.mean(grad_total * normed, axis=2, keepdims=True)
    grad_in = (cot_wide + inverse_rms * (grad_total - normed * projection_mean)).astype(
        jnp.bfloat16
    )
    return (grad_in, weight_sum, tap_part)


def mirrored(stacked):
    sections = lax.axis_size("section")
    pieces = stacked.reshape(
        stacked.shape[0], stacked.shape[1], sections, stacked.shape[2] // sections
    )
    spread = lax.all_to_all(pieces, "section", split_axis=2, concat_axis=2, tiled=True)
    collected = lax.all_to_all(
        jnp.flip(spread, 2), "section", split_axis=2, concat_axis=2, tiled=True
    )
    return collected.reshape(stacked.shape)


def per_device(weights, filters, down_input, down_cot, up_input, up_cot):
    weight_rows = weights[0]
    filter_taps = filters[0]
    tables = tap_tables(down_input.shape[1], filter_taps.shape[1])
    arriving = mirrored(jnp.stack([up_input[0], up_cot[0]], axis=1))
    up_inputs = arriving[:, 0:1]
    up_cotangent = arriving[:, 1:2]
    down_inputs = down_input[0][:, None]
    down_cotangent = down_cot[0][:, None]
    down_result, down_weight, down_taps = layer_grads(
        down_inputs, down_cotangent, weight_rows, filter_taps, tables
    )
    up_grad, up_weight, up_taps = layer_grads(
        up_inputs, up_cotangent, weight_rows, filter_taps, tables
    )
    down_grad = down_result[:, 0]
    weight_part = down_weight + up_weight
    tap_part = down_taps + up_taps
    taps_total = lax.psum(tap_part, "tensor")
    down_passed = shifted(down_grad, "section", -1)
    up_passed = shifted(mirrored(up_grad)[:, 0], "section", 1)
    return (
        weight_part.astype(jnp.bfloat16)[None],
        taps_total[None],
        down_passed[None],
        up_passed[None],
    )


def solution(mesh):
    in_specs = (
        P("section", "tensor", None),
        P("section", None, None),
        P("section", "tensor", None),
        P("section", "tensor", None),
        P("section", "tensor", None),
        P("section", "tensor", None),
    )
    out_specs = (
        P("section", "tensor", None),
        P("section", None, None),
        P("section", "tensor", None),
        P("section", "tensor", None),
    )
    return jax.shard_map(
        per_device, mesh=mesh, in_specs=in_specs, out_specs=out_specs, check_vma=False
    )
```

profile of v0, /device:TPU:0, one launch (start us, length us, event | category | flops | bytes accessed | tf_op | source)
XLA Modules:
  0.0 634.0 jit_solution(15924524114291938445)
XLA Ops:
  13.4 23.4 %reduce.5 = bf16[4096,128]{1,0:T(8,128)(2,1)} reduce(bf16[4096,1,128]{2,1,0:T(2,128)(2,1)S(1)} %bitcast.223, bf16[]{:T(256)} %broadcast.137), dimensions={1}, to_apply=%bitcast.182.reduce_sub_computation | reduce | bytes 2097154
  39.0 21.1 %all_to_all.68 = bf16[4,2,65536]{2,1,0:T(2,128)(2,1)} all-to-all(bf16[4,2,65536]{2,1,0:T(2,128)(2,1)S(1)} %reshape.472), channel_id=1, replica_groups=mesh['section'=32,'tensor'=4] {'tensor'}, dimensions={0} | all-to-all | bytes 2097152 | tf_op jit(solution)/shard_map/all_to_all | solution.py:41
  65.3 9.8 %fusion.26 = bf16[512,1,4096]{2,0,1:T(8,128)(2,1)} fusion(bf16[512,1024]{1,0:T(8,128)(2,1)S(1)} %bitcast.238, bf16[1,1024,4096]{2,1,0:T(8,128)(2,1)} %param.6), kind=kOutput, calls=%fused_computation.23 | convolution fusion | flops 4297064448 | bytes 13631488 | tf_op jit(solution)/shard_map/tmd,de->tme/dot_general | solution.py:44
  95.0 7.8 %all-to-all-start.1 = ((bf16[128,2,32,128]{0,3,1,2:T(8,128)(2,1)}), bf16[128,2,32,128]{0,3,1,2:T(8,128)(2,1)S(1)}, u32[]{:S(2)}, u32[]{:S(2)}) async-start(bf16[128,2,32,128]{0,3,1,2:T(8,128)(2,1)} %pad_maximum_fusion.1), calls=%async_computation.1 | async-start | bytes 4194304 | tf_op jit(solution)/shard_map/all_to_all | solution.py:88
  102.8 11.5 %all-gather.3.cloned.1.call-start = ((), (), s32[]{:S(2)}) async-start(), calls=%async_computation.10 | async-start | bytes 5242880 | tf_op jit(solution)/shard_map/all_gather | solution.py:66
  114.3 14.0 %fusion.40 = f32[32,128,255]{1,0,2:T(8,128)} fusion(s32[128,255]{0,1:T(8,128)S(1)} %iota_subtract_fusion.1, f32[1,32,128]{2,1,0:T(8,128)S(1)} %copy-done), kind=kOutput, calls=%fused_computation.42 | convolution fusion | flops 1608499200 | bytes 4324864 | tf_op jit(solution)/shard_map/tuk,gk->gtu/dot_general | solution.py:26
  139.3 8.7 %fusion.60 = bf16[32,128,128]{2,1,0:T(8,128)(2,1)} fusion(f32[32,128,255]{2,1,0:T(8,128)} %copy.101, f32[127,1,32,128]{0,3,2,1:T(8,128)} %bitcast.229, f32[128,1,32,128]{0,3,2,1:T(8,128)} %get-tuple-element.16), kind=kOutput, calls=%fused_computation.72 | convolution fusion | flops 1605890048 | bytes 9404416 | tf_op jit(solution)/shard_map/gtu,umgc->tmgc/dot_general | solution.py:28
  149.5 27.6 %all_to_all.69 = bf16[128,2,32,128]{0,3,1,2:T(8,128)(2,1)S(1)} all-to-all(bf16[128,2,32,128]{0,3,1,2:T(8,128)(2,1)} %rev.8), channel_id=1, replica_groups=mesh['section'=32,'tensor'=4] {'section'}, dimensions={2} | all-to-all | bytes 4194304 | tf_op jit(solution)/shard_map/all_to_all | solution.py:89
  179.6 17.0 %copy.134 = bf16[128,1,4096]{0,1,2:T(2,128)(2,1)} copy(bf16[128,1,4096]{0,2,1:T(8,128)(2,1)S(1)} %get-tuple-element.21) | data formatting | bytes 2097152 | tf_op jit(solution)/shard_map/convert_element_type | solution.py:40
  196.6 24.5 %reduce.6 = bf16[4096,128]{1,0:T(8,128)(2,1)} reduce(bf16[4096,1,128]{2,1,0:T(2,128)(2,1)} %bitcast.226, bf16[]{:T(256)} %broadcast.137), dimensions={1}, to_apply=%bitcast.203.reduce_sub_computation | reduce | bytes 2097154
  224.6 55.9 %all_to_all.70 = bf16[4,2,65536]{2,1,0:T(2,128)(2,1)} all-to-all(bf16[4,2,65536]{2,1,0:T(2,128)(2,1)} %reshape.474), channel_id=1, replica_groups=mesh['section'=32,'tensor'=4] {'tensor'}, dimensions={0} | all-to-all | bytes 2097152 | tf_op jit(solution)/shard_map/all_to_all | solution.py:41
  289.5 10.2 %fusion.23 = bf16[512,1,4096]{2,0,1:T(8,128)(2,1)} fusion(bf16[512,1024]{1,0:T(8,128)(2,1)} %bitcast.240, bf16[1,1024,4096]{2,1,0:T(8,128)(2,1)} %param.6), kind=kOutput, calls=%fused_computation.22 | convolution fusion | flops 4297064448 | bytes 13631488 | tf_op jit(solution)/shard_map/tmd,de->tme/dot_general | solution.py:44
  329.1 44.7 %collective-permute-start.2 = (bf16[127,1,4096]{2,0,1:T(8,128)(2,1)}, bf16[127,1,4096]{2,0,1:T(8,128)(2,1)}, u32[]{:S(2)}, u32[]{:S(2)}) collective-permute-start(bf16[127,1,4096]{2,0,1:T(8,128)(2,1)} %slice.31), channel_id=1, source_target_pairs={{0,1},{1,2},{2,3},{4,5},{5,6},{6,7},{8,9},{9,10},{10,11},{12,13},{... | collective-permute-start | bytes 3121160 | tf_op jit(solution)/shard_map/ppermute | solution.py:12
  373.8 10.4 %fusion.76 = bf16[512,1,1024]{2,0,1:T(8,128)(2,1)} fusion(bf16[1,1024,4096]{2,1,0:T(8,128)(2,1)} %param.6, bf16[512,1,4096]{0,2,1:T(8,128)(2,1)} %all-gather.3.cloned.1.call-done), kind=kOutput, calls=%fused_computation.77 | convolution fusion | flops 4295491584 | bytes 13631488 | tf_op jit(solution)/shard_map/tme,de->tmd/dot_general | solution.py:69
  395.5 14.0 %fusion.41 = f32[32,128,255]{1,0,2:T(8,128)} fusion(s32[128,255]{0,1:T(8,128)S(1)} %iota_subtract_fusion, f32[1,32,128]{2,1,0:T(8,128)S(1)} %copy-done), kind=kOutput, calls=%fused_computation.43 | convolution fusion | flops 1608499200 | bytes 4324864 | tf_op jit(solution)/shard_map/tuk,gk->gtu/dot_general | solution.py:26
  443.7 10.2 %fusion.71 = bf16[512,1,1024]{2,0,1:T(8,128)(2,1)} fusion(bf16[1,1024,4096]{2,1,0:T(8,128)(2,1)} %param.6, bf16[512,1,4096]{0,2,1:T(8,128)(2,1)} %all-gather.5.cloned.1.call-done), kind=kOutput, calls=%fused_computation.76 | convolution fusion | flops 4295491584 | bytes 13631488 | tf_op jit(solution)/shard_map/tme,de->tmd/dot_general | solution.py:69
  465.4 8.6 %fusion.54 = (f32[128]{0:T(128)S(1)}, f32[32,128,128]{2,1,0:T(8,128)}) fusion(f32[128,1,32,128]{0,3,2,1:T(8,128)} %bitcast.221, f32[128,1,32,128]{0,3,2,1:T(8,128)} %bitcast.211, f32[128,1,32,128]{0,3,2,1:T(8,128)} %bitcast.214, f32[128]{0:T(128)S(1)} %add_rsqrt_fusion.1, bf16[255,32,128]{0,2,1:T(8,128)(2,1)} %bitcast.219, f32[32,128,255]{2,1,0:T(8,128)} %copy.118), kind=kOutput, calls=%fused_computation.63 | convolution fusion | flops 1606942592 | bytes 14656512 | tf_op jit(solution)/shard_map/gtu,umgc->tmgc/dot_general | solution.py:28
  474.0 7.4 %all-to-all-done.5 = bf16[4,2,65536]{2,1,0:T(2,128)(2,1)} async-done(((bf16[4,2,65536]{2,1,0:T(2,128)(2,1)}), bf16[4,2,65536]{2,1,0:T(2,128)(2,1)}, u32[]{:S(2)}, u32[]{:S(2)}) %all-to-all-start.5) | async-done | bytes 1048608 | tf_op jit(solution)/shard_map/all_to_all | solution.py:72
  516.3 12.8 %all-to-all-done.6 = bf16[128,1,32,128]{0,3,1,2:T(8,128)(2,1)} async-done(((bf16[128,1,32,128]{0,3,1,2:T(8,128)(2,1)}), bf16[128,1,32,128]{0,3,1,2:T(8,128)(2,1)}, u32[]{:S(2)}, u32[]{:S(2)}) %all-to-all-start.6) | async-done | bytes 1048608 | tf_op jit(solution)/shard_map/all_to_all | solution.py:88
  536.9 10.5 %fusion.35 = f32[1024,4096]{1,0:T(8,128)} fusion(bf16[512,1024]{1,0:T(8,128)(2,1)S(1)} %bitcast.239, bf16[512,1,4096]{0,2,1:T(8,128)(2,1)} %all-gather.3.cloned.1.call-done), kind=kOutput, calls=%fused_computation.32 | convolution fusion | flops 4294967296 | bytes 22020096 | tf_op jit(solution)/shard_map/tmd,tme->de/dot_general | solution.py:68
  556.8 11.2 %fusion.81 = f32[32,128]{1,0:T(8,128)S(1)} fusion(f32[32,128,255]{1,0,2:T(8,128)} %copy.113, s32[128,255]{0,1:T(8,128)S(1)} %iota_subtract_fusion), kind=kOutput, calls=%fused_computation.78 | convolution fusion | flops 1608499200 | bytes 4324864 | tf_op jit(solution)/shard_map/gtu,tuk->gk/dot_general | solution.py:64
  577.5 11.4 %fusion.4 = bf16[1,1024,4096]{2,1,0:T(8,128)(2,1)} fusion(f32[1024,4096]{1,0:T(8,128)} %fusion.35, bf16[512,1024]{1,0:T(8,128)(2,1)S(1)} %bitcast.241, bf16[512,1,4096]{0,2,1:T(8,128)(2,1)} %all-gather.5.cloned.1.call-done), kind=kOutput, calls=%fused_computation.7 | convolution fusion | flops 4303355904 | bytes 30408704 | tf_op jit(solution)/shard_map/tmd,tme->de/dot_general | solution.py:68
  599.8 11.2 %fusion.84 = f32[1,32,128]{2,1,0:T(8,128)S(1)} fusion(f32[32,128]{1,0:T(8,128)S(1)} %fusion.81, f32[32,128,255]{1,0,2:T(8,128)} %copy.116, s32[128,255]{0,1:T(8,128)S(1)} %iota_subtract_fusion), kind=kOutput, calls=%fused_computation.81 | convolution fusion | flops 1608503296 | bytes 4341248 | tf_op jit(solution)/shard_map/gtu,tuk->gk/dot_general | solution.py:64
  611.0 13.7 %psum.7 = f32[1,32,128]{2,1,0:T(8,128)} all-reduce(f32[1,32,128]{2,1,0:T(8,128)S(1)} %fusion.84), channel_id=1, replica_groups=mesh['section'=32,'tensor'=4] {'tensor'}, use_global_device_ids=true, to_apply=%region_4.5 | all-reduce | flops 4096 | bytes 32768 | tf_op jit(solution)/shard_map/psum | solution.py:113
  (131 shorter events, 221.9 us)
Async XLA Ops:
  7.2 107.2 %copy-start = (f32[1,32,128]{2,1,0:T(8,128)S(1)}, f32[1,32,128]{2,1,0:T(8,128)}, u32[]{:S(2)}) copy-start(f32[1,32,128]{2,1,0:T(8,128)} %param.7) | copy-start | bytes 49156
  7.2 319.4 %reduce-scatter.3.cloned.1.call-start = ((), (), s32[]{:S(2)}) async-start(), calls=%async_computation.12 | async-start | bytes 5242880 | tf_op jit(solution)/shard_map/reduce_scatter | solution.py:43
  65.3 9.8 %copy-start.14 = (bf16[4,128,1,1024]{3,1,0,2:T(8,128)(2,1)}, bf16[4,128,1,1024]{3,1,0,2:T(8,128)(2,1)S(1)}, u32[]{:S(2)}) copy-start(bf16[4,128,1,1024]{3,1,0,2:T(8,128)(2,1)S(1)} %copy.97) | copy-start | bytes 3145732
  89.0 44.6 %collective-permute-start = (f32[127,1,4096]{2,1,0:T(1,128)}, f32[127,1,4096]{2,1,0:T(1,128)}, u32[]{:S(2)}, u32[]{:S(2)}) collective-permute-start(f32[127,1,4096]{2,1,0:T(1,128)} %copy.99), channel_id=1, source_target_pairs={{1,0},{2,1},{3,2},{5,4},{6,5},{7,6},{9,8},{10,9},{11,10},{13,12},{... | collective-permute-start | bytes 6242312 | tf_op jit(solution)/shard_map/ppermute | solution.py:12
  95.0 53.0 %all-to-all-start.1 = ((bf16[128,2,32,128]{0,3,1,2:T(8,128)(2,1)}), bf16[128,2,32,128]{0,3,1,2:T(8,128)(2,1)S(1)}, u32[]{:S(2)}, u32[]{:S(2)}) async-start(bf16[128,2,32,128]{0,3,1,2:T(8,128)(2,1)} %pad_maximum_fusion.1), calls=%async_computation.1 | async-start | bytes 4194304 | tf_op jit(solution)/shard_map/all_to_all | solution.py:88
  102.8 271.0 %all-gather.3.cloned.1.call-start = ((), (), s32[]{:S(2)}) async-start(), calls=%async_computation.10 | async-start | bytes 5242880 | tf_op jit(solution)/shard_map/all_gather | solution.py:66
  148.0 289.9 %reduce-scatter.5.cloned.1.call-start = ((), (), s32[]{:S(2)}) async-start(), calls=%async_computation.13 | async-start | bytes 5242880 | tf_op jit(solution)/shard_map/reduce_scatter | solution.py:43
  299.7 144.0 %all-gather.5.cloned.1.call-start = ((), (), s32[]{:S(2)}) async-start(), calls=%async_computation.11 | async-start | bytes 5242880 | tf_op jit(solution)/shard_map/all_gather | solution.py:66
  305.5 6.4 %collective-permute-start.1 = (f32[127,1,4096]{2,1,0:T(1,128)}, f32[127,1,4096]{2,1,0:T(1,128)}, u32[]{:S(2)}, u32[]{:S(2)}) collective-permute-start(f32[127,1,4096]{2,1,0:T(1,128)} %copy.107), channel_id=1, source_target_pairs={{1,0},{2,1},{3,2},{5,4},{6,5},{7,6},{9,8},{10,9},{11,10},{13,12},{... | collective-permute-start | bytes 6242312 | tf_op jit(solution)/shard_map/ppermute | solution.py:12
  329.1 101.5 %collective-permute-start.2 = (bf16[127,1,4096]{2,0,1:T(8,128)(2,1)}, bf16[127,1,4096]{2,0,1:T(8,128)(2,1)}, u32[]{:S(2)}, u32[]{:S(2)}) collective-permute-start(bf16[127,1,4096]{2,0,1:T(8,128)(2,1)} %slice.31), channel_id=1, source_target_pairs={{0,1},{1,2},{2,3},{4,5},{5,6},{6,7},{8,9},{9,10},{10,11},{12,13},{... | collective-permute-start | bytes 3121160 | tf_op jit(solution)/shard_map/ppermute | solution.py:12
  391.2 29.3 %all-to-all-start.4 = ((bf16[4,2,65536]{2,1,0:T(2,128)(2,1)}), bf16[4,2,65536]{2,1,0:T(2,128)(2,1)}, u32[]{:S(2)}, u32[]{:S(2)}) async-start(bf16[4,2,65536]{2,1,0:T(2,128)(2,1)} %reshape.476), calls=%async_computation.6 | async-start | bytes 2097152 | tf_op jit(solution)/shard_map/all_to_all | solution.py:72
  440.3 51.2 %collective-permute-start.3 = (bf16[127,1,4096]{2,0,1:T(8,128)(2,1)}, bf16[127,1,4096]{2,0,1:T(8,128)(2,1)}, u32[]{:S(2)}, u32[]{:S(2)}) collective-permute-start(bf16[127,1,4096]{2,0,1:T(8,128)(2,1)} %slice.32), channel_id=1, source_target_pairs={{0,1},{1,2},{2,3},{4,5},{5,6},{6,7},{8,9},{9,10},{10,11},{12,13},{... | collective-permute-start | bytes 3121160 | tf_op jit(solution)/shard_map/ppermute | solution.py:12
  460.9 20.5 %all-to-all-start.5 = ((bf16[4,2,65536]{2,1,0:T(2,128)(2,1)}), bf16[4,2,65536]{2,1,0:T(2,128)(2,1)}, u32[]{:S(2)}, u32[]{:S(2)}) async-start(bf16[4,2,65536]{2,1,0:T(2,128)(2,1)} %reshape.478), calls=%async_computation.7 | async-start | bytes 2097152 | tf_op jit(solution)/shard_map/all_to_all | solution.py:72
  506.3 22.8 %all-to-all-start.6 = ((bf16[128,1,32,128]{0,3,1,2:T(8,128)(2,1)}), bf16[128,1,32,128]{0,3,1,2:T(8,128)(2,1)}, u32[]{:S(2)}, u32[]{:S(2)}) async-start(bf16[128,1,32,128]{0,3,1,2:T(8,128)(2,1)} %bitcast.235), calls=%async_computation.8 | async-start | bytes 2097152 | tf_op jit(solution)/shard_map/all_to_all | solution.py:88
  514.9 22.0 %copy-start.15 = (bf16[4,128,1,1024]{3,1,0,2:T(8,128)(2,1)S(1)}, bf16[4,128,1,1024]{3,1,0,2:T(8,128)(2,1)}, u32[]{:S(2)}) copy-start(bf16[4,128,1,1024]{3,1,0,2:T(8,128)(2,1)} %copy-done.14) | copy-start | bytes 3145732
  514.9 53.1 %collective-permute-start.4 = (bf16[128,4096]{0,1:T(8,128)(2,1)}, bf16[128,4096]{0,1:T(8,128)(2,1)S(1)}, u32[]{:S(2)}, u32[]{:S(2)}) collective-permute-start(bf16[128,4096]{0,1:T(8,128)(2,1)} %fusion.51), channel_id=1, source_target_pairs={{4,0},{8,4},{12,8},{16,12},{20,16},{24,20},{28,24},{32,28},{36,32}... | collective-permute-start | bytes 3145736 | tf_op jit(solution)/shard_map/ppermute | solution.py:12
  531.4 39.9 %all-to-all-start.7 = ((bf16[128,1,32,128]{0,3,1,2:T(8,128)(2,1)}), bf16[128,1,32,128]{0,3,1,2:T(8,128)(2,1)S(1)}, u32[]{:S(2)}, u32[]{:S(2)}) async-start(bf16[128,1,32,128]{0,3,1,2:T(8,128)(2,1)} %rev.9), calls=%async_computation.9 | async-start | bytes 2097152 | tf_op jit(solution)/shard_map/all_to_all | solution.py:89
  536.9 10.6 %copy-start.7 = (bf16[255,1,4096]{0,2,1:T(8,128)(2,1)S(1)}, bf16[255,1,4096]{0,2,1:T(8,128)(2,1)}, u32[]{:S(2)}) copy-start(bf16[255,1,4096]{0,2,1:T(8,128)(2,1)} %copy.131) | copy-start | bytes 6266884
  536.9 10.5 %copy-start.11 = (f32[128,32,128]{2,0,1:T(8,128)S(1)}, f32[128,32,128]{2,0,1:T(8,128)}, u32[]{:S(2)}) copy-start(f32[128,32,128]{2,0,1:T(8,128)} %copy.111) | copy-start | bytes 6291460
  536.9 10.5 %copy-start.12 = (f32[128,32,128]{2,0,1:T(8,128)S(1)}, f32[128,32,128]{2,0,1:T(8,128)}, u32[]{:S(2)}) copy-start(f32[128,32,128]{2,0,1:T(8,128)} %copy.110) | copy-start | bytes 6291460
  569.0 8.6 %copy-start.16 = (bf16[4,128,1,1024]{3,1,0,2:T(8,128)(2,1)S(1)}, bf16[4,128,1,1024]{3,1,0,2:T(8,128)(2,1)}, u32[]{:S(2)}) copy-start(bf16[4,128,1,1024]{3,1,0,2:T(8,128)(2,1)} %copy.106) | copy-start | bytes 3145732
  572.6 16.3 %copy-start.5 = (f32[128,1,4096]{0,2,1:T(8,128)S(1)}, f32[128,1,4096]{0,2,1:T(8,128)}, u32[]{:S(2)}) copy-start(f32[128,1,4096]{0,2,1:T(8,128)} %get-tuple-element.20) | copy-start | bytes 6291460
  572.6 52.1 %collective-permute-start.5 = (bf16[128,4096]{1,0:T(8,128)(2,1)}, bf16[128,4096]{1,0:T(8,128)(2,1)}, u32[]{:S(2)}, u32[]{:S(2)}) collective-permute-start(bf16[128,4096]{1,0:T(8,128)(2,1)} %copy.126), channel_id=1, source_target_pairs={{0,4},{4,8},{8,12},{12,16},{16,20},{20,24},{24,28},{28,32},{32,36}... | collective-permute-start | bytes 3145736 | tf_op jit(solution)/shard_map/ppermute | solution.py:12
  599.8 27.2 %copy-start.1 = (f32[1,32,128]{2,1,0:T(8,128)S(1)}, f32[1,32,128]{2,1,0:T(8,128)}, u32[]{:S(2)}) copy-start(f32[1,32,128]{2,1,0:T(8,128)} %param.7) | copy-start | bytes 49156
  (9 other events, 25.7 us)
Sparse Core Ops, SparseCore 0:
  75.3 83.9 reduce-scatter.2
  161.6 73.2 all-gather.2
  299.8 58.0 reduce-scatter.4
  359.4 49.8 all-gather.4
where the time goes:
time: 645 us; the launch traced here: 634 us
  matrix products  150 us (23%)
  local copies, waits for them, and re-layouts  149 us (23%)
  blocking collectives  118 us (18%)
  starting transfers between devices  95.3 us (15%)
  other arithmetic  81.4 us (13%)
  waiting for transfers between devices  25.4 us (4%)
  between operations  14.6 us (2%)
    all_to_all x2, blocking collectives, layer_grads(): lax.all_to_all(normed_b, 'tensor', split_axis=2, concat_axis=0, tiled=True)  77 us
    ppermute x6, starting transfers between devices, shifted(): return lax.ppermute(x, axis, pairs)  56.9 us
    unnamed x2, other arithmetic  47.8 us
    unnamed x53, local copies, waits for them, and re-layouts  46.8 us
    dot_general x2, matrix products, banded(): jnp.einsum('tuk,gk->gtu', table, filter_taps, precision=lax.Precision.HIG...  28 us
    dot_general x4, matrix products, banded(): jnp.einsum('gtu,umgc->tmgc', band, grouped, precision=lax.Precision.HIGHEST)  27.8 us
    all_to_all x1, blocking collectives, mirrored(): lax.all_to_all(jnp.flip(spread, 2), 'section', split_axis=2, concat_axis=...  27.6 us
    dot_general x2, matrix products, layer_grads(): jnp.einsum('gtu,tuk->gk', pairs, causal_table, precision=lax.Precision.HI...  22.3 us
  transfers between devices with their start and end apart: 15, of which 3 were waited for; matrix products, arithmetic and copies ran while one was open for 49% of the time, Pallas kernels for 0%

commit v1 on v0

--- a/solution.py
+++ b/solution.py
@@ -38,7 +38,15 @@
     inverse_rms = lax.rsqrt(jnp.mean(input_wide * input_wide, axis=2, keepdims=True) + epsilon)
     normed = input_wide * inverse_rms
     normed_b = normed.astype(jnp.bfloat16)
-    feature_rows = lax.all_to_all(normed_b, "tensor", split_axis=2, concat_axis=0, tiled=True)
+
+    def fill_the_panel(block_in):
+        piece_now = lax.axis_size("tensor")
+        arr_now = jnp.split(block_in, piece_now, axis=2)
+        part_next = jnp.stack(arr_now, axis=0)
+        answer = lax.all_to_all(part_next, "tensor", 0, 0)
+        return jnp.concatenate(answer, axis=0)
+
+    feature_rows = fill_the_panel(normed_b)
     selected = feature_rows
     values = lax.psum_scatter(
         jnp.einsum("tmd,de->tme", selected, weight_rows, preferred_element_type=jnp.float32).astype(

time: 645 us -> 545 us (0.84)
  other arithmetic: 81.4 us -> 35.9 us
  local copies, waits for them, and re-layouts: 149 us -> 123 us
  starting transfers between devices: 95.3 us -> 78.8 us
    unnamed x2, other arithmetic: 47.8 us -> 1.78 us
    convert_element_type x1, local copies, waits for them, and re-layouts: 17 us -> 0.51 us  [layer_grads(): returned_rows.astype(jnp.bfloat16)]
    unnamed x53 -> x50, local copies, waits for them, and re-layouts: 46.8 us -> 30.9 us
    ppermute x6, starting transfers between devices: 56.9 us -> 45.2 us  [shifted(): return lax.ppermute(x, axis, pairs)]
    all_gather x2, starting transfers between devices: 11.6 us -> 0.3 us  [layer_grads(): shard_rows = lax.all_gather(grad_values_b, 'tensor', axis=0, tiled=True)]
    another operation x3 -> x6, local copies, waits for them, and re-layouts: 9.45 us -> 13.3 us
    convert_element_type x2 -> x3, local copies, waits for them, and re-layouts: 12.2 us -> 15.1 us  [layer_grads(): back_tokens = lax.all_to_all(returned_rows.astype(jnp.bfloat16), 'tensor'...]
  transfers between devices with their start and end apart: 15 -> 15, of which waited for: 3 -> 4; matrix products, arithmetic and copies ran while one was open for 49% -> 50% of each run, Pallas kernels for 0% -> 0%
where the time goes in v1:
time: 545 us; the launch traced here: 536 us
  matrix products  147 us (27%)
  local copies, waits for them, and re-layouts  123 us (23%)
  blocking collectives  115 us (21%)
  starting transfers between devices  78.8 us (14%)
  other arithmetic  35.9 us (7%)
  waiting for transfers between devices  22.1 us (4%)
  between operations  14.7 us (3%)
    all_to_all x2, blocking collectives, fill_the_panel(): answer = lax.all_to_all(part_next, 'tensor', 0, 0)  74 us
    ppermute x6, starting transfers between devices, shifted(): return lax.ppermute(x, axis, pairs)  45.2 us
    unnamed x50, local copies, waits for them, and re-layouts  30.9 us
    dot_general x2, matrix products, banded(): jnp.einsum('tuk,gk->gtu', table, filter_taps, precision=lax.Precision.HIG...  28 us
    all_to_all x1, blocking collectives, mirrored(): lax.all_to_all(jnp.flip(spread, 2), 'section', split_axis=2, concat_axis=...  27.4 us
    dot_general x4, matrix products, banded(): jnp.einsum('gtu,umgc->tmgc', band, grouped, precision=lax.Precision.HIGHEST)  27.2 us
    dot_general x2, matrix products, layer_grads(): jnp.einsum('gtu,tuk->gk', pairs, causal_table, precision=lax.Precision.HI...  22.3 us
    dot_general x2, matrix products, layer_grads(): jnp.einsum('tmd,tme->de', selected, shard_rows, preferred_element_type=jn...  21.9 us
  transfers between devices with their start and end apart: 15, of which 4 were waited for; matrix products, arithmetic and copies ran while one was open for 50% of the time, Pallas kernels for 0%

profile of v1, /device:TPU:0, one launch (start us, length us, event | category | flops | bytes accessed | tf_op | source)
XLA Modules:
  0.0 536.4 jit_solution(1531002002552755778)
XLA Ops:
  10.7 21.1 %all_to_all.48 = bf16[4,128,1,1024]{3,1,2,0:T(8,128)(2,1)S(1)} all-to-all(bf16[4,128,1,1024]{3,1,2,0:T(8,128)(2,1)S(1)} %pad_maximum_fusion.4), channel_id=1, replica_groups=mesh['section'=32,'tensor'=4] {'tensor'}, dimensions={0} | all-to-all | bytes 2097152 | tf_op jit(solution)/shard_map/all_to_all | solution.py:46
  32.8 6.1 %fusion.26 = bf16[512,1,4096]{2,0,1:T(8,128)(2,1)} fusion(bf16[512,1024]{1,0:T(8,128)(2,1)S(1)} %bitcast.240, bf16[1,1024,4096]{2,1,0:T(8,128)(2,1)S(1)} %copy-done.19), kind=kOutput, calls=%fused_computation.23 | convolution fusion | flops 4297064448 | bytes 13631488 | tf_op jit(solution)/shard_map/tmd,de->tme/dot_general | solution.py:52
  53.2 7.9 %all-to-all-start.1 = ((bf16[128,2,32,128]{3,0,1,2:T(8,128)(2,1)}), bf16[128,2,32,128]{3,0,1,2:T(8,128)(2,1)}, u32[]{:S(2)}, u32[]{:S(2)}) async-start(bf16[128,2,32,128]{3,0,1,2:T(8,128)(2,1)} %copy.82), calls=%async_computation.1 | async-start | bytes 4194304 | tf_op jit(solution)/shard_map/all_to_all | solution.py:96
  64.8 14.0 %fusion.40 = f32[32,128,255]{1,0,2:T(8,128)} fusion(s32[128,255]{0,1:T(8,128)S(1)} %iota_subtract_fusion.1, f32[1,32,128]{2,1,0:T(8,128)S(1)} %copy-done), kind=kOutput, calls=%fused_computation.42 | convolution fusion | flops 1608499200 | bytes 4324864 | tf_op jit(solution)/shard_map/tuk,gk->gtu/dot_general | solution.py:26
  93.1 8.0 %fusion.59 = bf16[32,128,128]{2,1,0:T(8,128)(2,1)} fusion(f32[32,128,255]{2,1,0:T(8,128)} %copy.79, f32[127,1,32,128]{0,3,2,1:T(8,128)} %bitcast.233, f32[128,1,32,128]{0,3,2,1:T(8,128)S(1)} %copy-done.10), kind=kOutput, calls=%fused_computation.76 | convolution fusion | flops 1605890048 | bytes 9404416 | tf_op jit(solution)/shard_map/gtu,umgc->tmgc/dot_general | solution.py:28
  103.0 27.4 %all_to_all.49 = bf16[128,2,32,128]{3,0,1,2:T(8,128)(2,1)} all-to-all(bf16[128,2,32,128]{3,0,1,2:T(8,128)(2,1)S(1)} %rev.8), channel_id=1, replica_groups=mesh['section'=32,'tensor'=4] {'section'}, dimensions={2} | all-to-all | bytes 4194304 | tf_op jit(solution)/shard_map/all_to_all | solution.py:97
  139.3 52.9 %all_to_all.50 = bf16[4,128,1,1024]{3,1,2,0:T(8,128)(2,1)S(1)} all-to-all(bf16[4,128,1,1024]{3,1,2,0:T(8,128)(2,1)} %copy.84), channel_id=1, replica_groups=mesh['section'=32,'tensor'=4] {'tensor'}, dimensions={0} | all-to-all | bytes 2097152 | tf_op jit(solution)/shard_map/all_to_all | solution.py:46
  193.2 9.5 %fusion.23 = bf16[512,1,4096]{2,0,1:T(8,128)(2,1)} fusion(bf16[512,1024]{1,0:T(8,128)(2,1)S(1)} %bitcast.242, bf16[1,1024,4096]{2,1,0:T(8,128)(2,1)} %param.6), kind=kOutput, calls=%fused_computation.22 | convolution fusion | flops 4297064448 | bytes 13631488 | tf_op jit(solution)/shard_map/tmd,de->tme/dot_general | solution.py:52
  232.0 32.7 %collective-permute-start.2 = (bf16[127,1,4096]{2,0,1:T(8,128)(2,1)}, bf16[127,1,4096]{2,0,1:T(8,128)(2,1)}, u32[]{:S(2)}, u32[]{:S(2)}) collective-permute-start(bf16[127,1,4096]{2,0,1:T(8,128)(2,1)} %slice.31), channel_id=1, source_target_pairs={{0,1},{1,2},{2,3},{4,5},{5,6},{6,7},{8,9},{9,10},{10,11},{12,13},{... | collective-permute-start | bytes 3121160 | tf_op jit(solution)/shard_map/ppermute | solution.py:12
  264.7 10.2 %fusion.75 = bf16[512,1,1024]{2,0,1:T(8,128)(2,1)} fusion(bf16[1,1024,4096]{2,1,0:T(8,128)(2,1)} %param.6, bf16[512,1,4096]{0,2,1:T(8,128)(2,1)} %all-gather.3.cloned.1.call-done), kind=kOutput, calls=%fused_computation.81 | convolution fusion | flops 4295491584 | bytes 13631488 | tf_op jit(solution)/shard_map/tme,de->tmd/dot_general | solution.py:77
  286.9 14.0 %fusion.41 = f32[32,128,255]{1,0,2:T(8,128)} fusion(s32[128,255]{0,1:T(8,128)S(1)} %iota_subtract_fusion, f32[1,32,128]{2,1,0:T(8,128)S(1)} %copy-done), kind=kOutput, calls=%fused_computation.43 | convolution fusion | flops 1608499200 | bytes 4324864 | tf_op jit(solution)/shard_map/tuk,gk->gtu/dot_general | solution.py:26
  315.7 6.1 %copy.99 = f32[4,128,1,1024]{1,3,0,2:T(8,128)} copy(bf16[4,128,1,1024]{3,2,1,0:T(2,128)(2,1)} %bitcast.229) | data formatting | bytes 3145728 | tf_op jit(solution)/shard_map/convert_element_type | solution.py:82
  337.4 10.2 %fusion.70 = bf16[512,1,1024]{2,0,1:T(8,128)(2,1)} fusion(bf16[1,1024,4096]{2,1,0:T(8,128)(2,1)} %param.6, bf16[512,1,4096]{0,2,1:T(8,128)(2,1)} %all-gather.5.cloned.1.call-done), kind=kOutput, calls=%fused_computation.80 | convolution fusion | flops 4295491584 | bytes 13631488 | tf_op jit(solution)/shard_map/tme,de->tmd/dot_general | solution.py:77
  359.2 8.6 %fusion.50 = (f32[128]{0:T(128)S(1)}, f32[32,128,128]{2,1,0:T(8,128)}) fusion(f32[128,1,32,128]{0,3,2,1:T(8,128)} %bitcast.225, f32[128,1,32,128]{0,3,2,1:T(8,128)} %bitcast.220, f32[128,1,32,128]{0,3,2,1:T(8,128)} %bitcast.221, f32[128]{0:T(128)S(1)} %add_rsqrt_fusion.1, bf16[255,32,128]{0,2,1:T(8,128)(2,1)} %bitcast.226, f32[32,128,255]{2,1,0:T(8,128)} %copy.96), kind=kOutput, calls=%fused_computation.57 | convolution fusion | flops 1606942592 | bytes 14656512 | tf_op jit(solution)/shard_map/gtu,umgc->tmgc/dot_general | solution.py:28
  379.2 6.1 %copy.104 = f32[4,128,1,1024]{1,3,0,2:T(8,128)} copy(bf16[4,128,1,1024]{3,2,1,0:T(2,128)(2,1)} %bitcast.230) | data formatting | bytes 3145728 | tf_op jit(solution)/shard_map/convert_element_type | solution.py:82
  402.6 9.8 %all-to-all-start.6 = ((bf16[128,1,32,128]{3,0,1,2:T(8,128)(2,1)}), bf16[128,1,32,128]{3,0,1,2:T(8,128)(2,1)S(1)}, u32[]{:S(2)}, u32[]{:S(2)}) async-start(bf16[128,1,32,128]{3,0,1,2:T(8,128)(2,1)} %copy.105), calls=%async_computation.8 | async-start | bytes 2097152 | tf_op jit(solution)/shard_map/all_to_all | solution.py:96
  417.8 12.3 %all-to-all-done.6 = bf16[128,1,32,128]{3,0,1,2:T(8,128)(2,1)S(1)} async-done(((bf16[128,1,32,128]{3,0,1,2:T(8,128)(2,1)}), bf16[128,1,32,128]{3,0,1,2:T(8,128)(2,1)S(1)}, u32[]{:S(2)}, u32[]{:S(2)}) %all-to-all-start.6) | async-done | bytes 1048608 | tf_op jit(solution)/shard_map/all_to_all | solution.py:96
  431.2 6.5 %all-to-all-start.7 = ((bf16[128,1,32,128]{3,0,1,2:T(8,128)(2,1)}), bf16[128,1,32,128]{3,0,1,2:T(8,128)(2,1)S(1)}, u32[]{:S(2)}, u32[]{:S(2)}) async-start(bf16[128,1,32,128]{3,0,1,2:T(8,128)(2,1)} %rev.9), calls=%async_computation.9 | async-start | bytes 2097152 | tf_op jit(solution)/shard_map/all_to_all | solution.py:97
  437.8 10.5 %fusion.35 = f32[1024,4096]{1,0:T(8,128)} fusion(bf16[512,1024]{1,0:T(8,128)(2,1)S(1)} %bitcast.241, bf16[512,1,4096]{0,2,1:T(8,128)(2,1)} %all-gather.3.cloned.1.call-done), kind=kOutput, calls=%fused_computation.32 | convolution fusion | flops 4294967296 | bytes 22020096 | tf_op jit(solution)/shard_map/tmd,tme->de/dot_general | solution.py:76
  448.3 6.1 %fusion.58 = f32[32,128,255]{2,1,0:T(8,128)} fusion(bf16[255,32,128]{0,2,1:T(8,128)(2,1)S(1)} %bitcast.227, f32[128,32,128]{2,1,0:T(8,128)S(1)} %bitcast.231, f32[128,32,128]{2,1,0:T(8,128)S(1)} %bitcast.232, f32[128]{0:T(128)S(1)} %add_rsqrt_fusion.1), kind=kOutput, calls=%fused_computation.70 | convolution fusion | flops 1605369856 | bytes 10461696 | tf_op jit(solution)/shard_map/tmgc,umgc->gtu/dot_general | solution.py:71
  459.8 11.2 %fusion.80 = f32[32,128]{1,0:T(8,128)S(1)} fusion(f32[32,128,255]{1,0,2:T(8,128)} %copy.91, s32[128,255]{0,1:T(8,128)S(1)} %iota_subtract_fusion), kind=kOutput, calls=%fused_computation.82 | convolution fusion | flops 1608499200 | bytes 4324864 | tf_op jit(solution)/shard_map/gtu,tuk->gk/dot_general | solution.py:72
  477.6 11.4 %fusion.4 = bf16[1,1024,4096]{2,1,0:T(8,128)(2,1)} fusion(f32[1024,4096]{1,0:T(8,128)} %fusion.35, bf16[512,1024]{1,0:T(8,128)(2,1)S(1)} %bitcast.243, bf16[512,1,4096]{0,2,1:T(8,128)(2,1)} %all-gather.5.cloned.1.call-done), kind=kOutput, calls=%fused_computation.7 | convolution fusion | flops 4303355904 | bytes 30408704 | tf_op jit(solution)/shard_map/tmd,tme->de/dot_general | solution.py:76
  499.9 11.2 %fusion.83 = f32[1,32,128]{2,1,0:T(8,128)S(1)} fusion(f32[32,128]{1,0:T(8,128)S(1)} %fusion.80, f32[32,128,255]{1,0,2:T(8,128)} %copy.94, s32[128,255]{0,1:T(8,128)S(1)} %iota_subtract_fusion), kind=kOutput, calls=%fused_computation.85 | convolution fusion | flops 1608503296 | bytes 4341248 | tf_op jit(solution)/shard_map/gtu,tuk->gk/dot_general | solution.py:72
  511.1 13.7 %psum.7 = f32[1,32,128]{2,1,0:T(8,128)} all-reduce(f32[1,32,128]{2,1,0:T(8,128)S(1)} %fusion.83), channel_id=1, replica_groups=mesh['section'=32,'tensor'=4] {'tensor'}, use_global_device_ids=true, to_apply=%region_4.5 | all-reduce | flops 4096 | bytes 32768 | tf_op jit(solution)/shard_map/psum | solution.py:121
  (134 shorter events, 194.3 us)
Async XLA Ops:
  7.2 57.7 %copy-start = (f32[1,32,128]{2,1,0:T(8,128)S(1)}, f32[1,32,128]{2,1,0:T(8,128)}, u32[]{:S(2)}) copy-start(f32[1,32,128]{2,1,0:T(8,128)} %param.7) | copy-start | bytes 49156
  7.2 222.3 %reduce-scatter.3.cloned.1.call-start = ((), (), s32[]{:S(2)}) async-start(), calls=%async_computation.12 | async-start | bytes 5242880 | tf_op jit(solution)/shard_map/reduce_scatter | solution.py:51
  8.8 24.1 %copy-start.19 = (bf16[1,1024,4096]{2,1,0:T(8,128)(2,1)S(1)}, bf16[1,1024,4096]{2,1,0:T(8,128)(2,1)}, u32[]{:S(2)}) copy-start(bf16[1,1024,4096]{2,1,0:T(8,128)(2,1)} %param.6) | copy-start | bytes 25165828
  45.5 41.9 %collective-permute-start = (f32[127,1,4096]{2,1,0:T(1,128)}, f32[127,1,4096]{2,1,0:T(1,128)}, u32[]{:S(2)}, u32[]{:S(2)}) collective-permute-start(f32[127,1,4096]{2,1,0:T(1,128)} %copy.77), channel_id=1, source_target_pairs={{1,0},{2,1},{3,2},{5,4},{6,5},{7,6},{9,8},{10,9},{11,10},{13,12},{... | collective-permute-start | bytes 6242312 | tf_op jit(solution)/shard_map/ppermute | solution.py:12
  53.2 48.0 %all-to-all-start.1 = ((bf16[128,2,32,128]{3,0,1,2:T(8,128)(2,1)}), bf16[128,2,32,128]{3,0,1,2:T(8,128)(2,1)}, u32[]{:S(2)}, u32[]{:S(2)}) async-start(bf16[128,2,32,128]{3,0,1,2:T(8,128)(2,1)} %copy.82), calls=%async_computation.1 | async-start | bytes 4194304 | tf_op jit(solution)/shard_map/all_to_all | solution.py:96
  61.1 203.6 %all-gather.3.cloned.1.call-start = ((), (), s32[]{:S(2)}) async-start(), calls=%async_computation.10 | async-start | bytes 5242880 | tf_op jit(solution)/shard_map/all_gather | solution.py:74
  62.9 21.2 %copy-start.6 = (f32[1,128,4096]{1,2,0:T(8,128)}, f32[1,128,4096]{1,2,0:T(8,128)S(1)}, u32[]{:S(2)}) copy-start(f32[1,128,4096]{1,2,0:T(8,128)S(1)} %copy.75) | copy-start | bytes 6291460
  101.2 230.8 %reduce-scatter.5.cloned.1.call-start = ((), (), s32[]{:S(2)}) async-start(), calls=%async_computation.13 | async-start | bytes 5242880 | tf_op jit(solution)/shard_map/reduce_scatter | solution.py:51
  202.6 134.8 %all-gather.5.cloned.1.call-start = ((), (), s32[]{:S(2)}) async-start(), calls=%async_computation.11 | async-start | bytes 5242880 | tf_op jit(solution)/shard_map/all_gather | solution.py:74
  208.4 6.5 %collective-permute-start.1 = (f32[127,1,4096]{2,1,0:T(1,128)}, f32[127,1,4096]{2,1,0:T(1,128)}, u32[]{:S(2)}, u32[]{:S(2)}) collective-permute-start(f32[127,1,4096]{2,1,0:T(1,128)} %copy.85), channel_id=1, source_target_pairs={{1,0},{2,1},{3,2},{5,4},{6,5},{7,6},{9,8},{10,9},{11,10},{13,12},{... | collective-permute-start | bytes 6242312 | tf_op jit(solution)/shard_map/ppermute | solution.py:12
  232.0 92.7 %collective-permute-start.2 = (bf16[127,1,4096]{2,0,1:T(8,128)(2,1)}, bf16[127,1,4096]{2,0,1:T(8,128)(2,1)}, u32[]{:S(2)}, u32[]{:S(2)}) collective-permute-start(bf16[127,1,4096]{2,0,1:T(8,128)(2,1)} %slice.31), channel_id=1, source_target_pairs={{0,1},{1,2},{2,3},{4,5},{5,6},{6,7},{8,9},{9,10},{10,11},{12,13},{... | collective-permute-start | bytes 3121160 | tf_op jit(solution)/shard_map/ppermute | solution.py:12
  282.4 29.3 %all-to-all-start.4 = ((bf16[4,2,65536]{2,1,0:T(2,128)(2,1)}), bf16[4,2,65536]{2,1,0:T(2,128)(2,1)}, u32[]{:S(2)}, u32[]{:S(2)}) async-start(bf16[4,2,65536]{2,1,0:T(2,128)(2,1)} %reshape.474), calls=%async_computation.6 | async-start | bytes 2097152 | tf_op jit(solution)/shard_map/all_to_all | solution.py:80
  334.5 50.9 %collective-permute-start.3 = (bf16[127,1,4096]{2,0,1:T(8,128)(2,1)}, bf16[127,1,4096]{2,0,1:T(8,128)(2,1)}, u32[]{:S(2)}, u32[]{:S(2)}) collective-permute-start(bf16[127,1,4096]{2,0,1:T(8,128)(2,1)} %slice.32), channel_id=1, source_target_pairs={{0,1},{1,2},{2,3},{4,5},{5,6},{6,7},{8,9},{9,10},{10,11},{12,13},{... | collective-permute-start | bytes 3121160 | tf_op jit(solution)/shard_map/ppermute | solution.py:12
  354.7 20.5 %all-to-all-start.5 = ((bf16[4,2,65536]{2,1,0:T(2,128)(2,1)}), bf16[4,2,65536]{2,1,0:T(2,128)(2,1)}, u32[]{:S(2)}, u32[]{:S(2)}) async-start(bf16[4,2,65536]{2,1,0:T(2,128)(2,1)} %reshape.476), calls=%async_computation.7 | async-start | bytes 2097152 | tf_op jit(solution)/shard_map/all_to_all | solution.py:80
  400.2 12.2 %copy-start.9 = (bf16[1,128,4096]{2,1,0:T(8,128)(2,1)S(1)}, bf16[1,128,4096]{2,1,0:T(8,128)(2,1)}, u32[]{:S(2)}) copy-start(bf16[1,128,4096]{2,1,0:T(8,128)(2,1)} %param.9) | copy-start | bytes 3145732
  402.6 27.6 %all-to-all-start.6 = ((bf16[128,1,32,128]{3,0,1,2:T(8,128)(2,1)}), bf16[128,1,32,128]{3,0,1,2:T(8,128)(2,1)S(1)}, u32[]{:S(2)}, u32[]{:S(2)}) async-start(bf16[128,1,32,128]{3,0,1,2:T(8,128)(2,1)} %copy.105), calls=%async_computation.8 | async-start | bytes 2097152 | tf_op jit(solution)/shard_map/all_to_all | solution.py:96
  416.4 21.4 %copy-start.16 = (bf16[4,128,1,1024]{3,1,2,0:T(8,128)(2,1)S(1)}, bf16[4,128,1,1024]{3,1,2,0:T(8,128)(2,1)}, u32[]{:S(2)}) copy-start(bf16[4,128,1,1024]{3,1,2,0:T(8,128)(2,1)} %copy-done.15) | copy-start | bytes 3145732
  416.4 54.6 %collective-permute-start.4 = (bf16[128,4096]{1,0:T(8,128)(2,1)}, bf16[128,4096]{1,0:T(8,128)(2,1)}, u32[]{:S(2)}, u32[]{:S(2)}) collective-permute-start(bf16[128,4096]{1,0:T(8,128)(2,1)} %fusion.55), channel_id=1, source_target_pairs={{4,0},{8,4},{12,8},{16,12},{20,16},{24,20},{28,24},{32,28},{36,32}... | collective-permute-start | bytes 3145736 | tf_op jit(solution)/shard_map/ppermute | solution.py:12
  431.2 39.8 %all-to-all-start.7 = ((bf16[128,1,32,128]{3,0,1,2:T(8,128)(2,1)}), bf16[128,1,32,128]{3,0,1,2:T(8,128)(2,1)S(1)}, u32[]{:S(2)}, u32[]{:S(2)}) async-start(bf16[128,1,32,128]{3,0,1,2:T(8,128)(2,1)} %rev.9), calls=%async_computation.9 | async-start | bytes 2097152 | tf_op jit(solution)/shard_map/all_to_all | solution.py:97
  437.8 10.5 %copy-start.7 = (bf16[255,1,4096]{0,2,1:T(8,128)(2,1)S(1)}, bf16[255,1,4096]{0,2,1:T(8,128)(2,1)}, u32[]{:S(2)}) copy-start(bf16[255,1,4096]{0,2,1:T(8,128)(2,1)} %copy.110) | copy-start | bytes 6266884
  437.8 10.5 %copy-start.11 = (f32[16,8,32,128]{3,2,1,0:T(8,128)S(1)}, f32[16,8,32,128]{3,2,1,0:T(8,128)}, u32[]{:S(2)}) copy-start(f32[16,8,32,128]{3,2,1,0:T(8,128)} %copy.112) | copy-start | bytes 6291460
  437.8 10.5 %copy-start.12 = (f32[16,8,32,128]{3,2,1,0:T(8,128)S(1)}, f32[16,8,32,128]{3,2,1,0:T(8,128)}, u32[]{:S(2)}) copy-start(f32[16,8,32,128]{3,2,1,0:T(8,128)} %copy.113) | copy-start | bytes 6291460
  472.3 16.7 %copy-start.3 = (f32[128,1,4096]{0,2,1:T(8,128)S(1)}, f32[128,1,4096]{0,2,1:T(8,128)}, u32[]{:S(2)}) copy-start(f32[128,1,4096]{0,2,1:T(8,128)} %get-tuple-element.8) | copy-start | bytes 6291460
  472.3 52.4 %collective-permute-start.5 = (bf16[128,4096]{0,1:T(8,128)(2,1)}, bf16[128,4096]{0,1:T(8,128)(2,1)}, u32[]{:S(2)}, u32[]{:S(2)}) collective-permute-start(bf16[128,4096]{0,1:T(8,128)(2,1)} %bitcast.244), channel_id=1, source_target_pairs={{0,4},{4,8},{8,12},{12,16},{16,20},{20,24},{24,28},{28,32},{32,36}... | collective-permute-start | bytes 3145736 | tf_op jit(solution)/shard_map/ppermute | solution.py:12
  (11 other events, 40.9 us)
Sparse Core Ops, SparseCore 0:
  39.1 92.4 reduce-scatter.2
  133.9 51.4 all-gather.2
  202.8 59.4 reduce-scatter.4
  263.7 47.7 all-gather.4
